TPU v7x, 32 devices: a whole 2x2x4 slice. The times are simulated.
32 devices in a mesh: dp: 4 (over y, core), lat: 8 (over z, x).
Axes of the slice: x: 2, y: 2, z: 4, core: 2. Of those that a mesh axis runs over, the one named last changes fastest.
Arguments:
- inputs: bfloat16 [4, 96, 180, 768], P('dp', 'lat'), may hold values from -6 to 6
- cotangent: bfloat16 [4, 96, 180, 768], P('dp', 'lat'), may hold values from -6 to 6
- storm_weight: int32 [4], P('dp'), may hold values from 32 to 192
- norm_gain: float32 [768], replicated, may hold values from 0.5 to 1.5
- norm_shift: float32 [768], replicated, may hold values from -1 to 1
- inner_weight: bfloat16 [2, 8, 96, 96], replicated, may hold values from -0.4375 to 0.4375
- inner_bias: float32 [2, 8, 96], replicated, may hold values from -0.1 to 0.1
- outer_weight: bfloat16 [2, 8, 96, 96], replicated, may hold values from -0.4375 to 0.4375
- outer_bias: float32 [2, 8, 96], replicated, may hold values from -0.05 to 0.05
- post_gain: float32 [768], replicated, may hold values from 0.5 to 1.5
- post_shift: float32 [768], replicated, may hold values from -1 to 1
- expand_weight: bfloat16 [768, 3072], replicated, may hold values from -0.21875 to 0.21875
- expand_bias: float32 [3072], replicated, may hold values from -0.5 to 0.5
- reduce_weight: bfloat16 [3072, 768], replicated, may hold values from -0.109375 to 0.109375
- reduce_bias: float32 [768], replicated, may hold values from -0.5 to 0.5
Outputs:
- layer_out: bfloat16 [4, 96, 180, 768], P('dp', 'lat')
- input_grad: float32 [4, 96, 180, 768], P('dp', 'lat')
- norm_gain_grad: float32 [768], replicated
- norm_shift_grad: float32 [768], replicated
- inner_weight_grad: float32 [2, 8, 96, 96], replicated
- inner_bias_grad: float32 [2, 8, 96], replicated
- outer_weight_grad: float32 [2, 8, 96, 96], replicated
- outer_bias_grad: float32 [2, 8, 96], replicated
- post_gain_grad: float32 [768], replicated
- post_shift_grad: float32 [768], replicated
- expand_weight_grad: float32 [768, 3072], replicated
- expand_bias_grad: float32 [3072], replicated
- reduce_weight_grad: float32 [3072, 768], replicated
- reduce_bias_grad: float32 [768], replicated
All inputs are finite; a program needn't handle non-finite values.
Results may differ from a plain program's by a relative error of at most 0.017.
The roundings to bfloat16 on the way count: a program that leaves them out, or rounds other values in their place, can miss the bound.
Values may be sent and summed in bfloat16 or wider, within the bound.
A program may use at most 320 MiB of HBM per device.

v0:
```python
from functools import partial
import math
import jax
import jax.numpy as jnp
from jax import lax
from jax.sharding import PartitionSpec as P

BLOCKS = 8
LAT = 90
LON = 180
LAT_PAD = 96
LON_PAD = 96
shrink_level = 0.01
epsilon = 1e-06


def make_tables():
    mode_ids = jnp.arange(LON_PAD, dtype=jnp.int32)
    columns = jnp.arange(LON, dtype=jnp.int32)
    phases = (columns[:, None] * mode_ids[None, :] % LON).astype(jnp.float32) * (
        2.0 * math.pi / LON
    )
    kept_modes = (mode_ids < LON // 2 + 1).astype(jnp.float32)
    factor = (
        jnp.where((mode_ids == 0) | (mode_ids == LON // 2), 1.0, 2.0).astype(jnp.float32)
        * kept_modes
    )
    scaling = 1.0 / math.sqrt(LON)
    forward_lon = (
        jnp.stack([jnp.cos(phases) * kept_modes, -jnp.sin(phases) * kept_modes], axis=1) * scaling
    )
    inverse_lon = jnp.stack([jnp.cos(phases) * factor, -jnp.sin(phases) * factor], axis=1) * scaling
    row_ids = jnp.arange(LAT_PAD, dtype=jnp.int32)
    angles = (row_ids[:, None] * row_ids[None, :] % LAT).astype(jnp.float32) * (2.0 * math.pi / LAT)
    inside = ((row_ids[:, None] < LAT) & (row_ids[None, :] < LAT)).astype(jnp.float32) / math.sqrt(
        LAT
    )
    cosine = jnp.cos(angles) * inside
    sine_part = jnp.sin(angles) * inside
    forward_lat = jnp.stack(
        [jnp.stack([cosine, sine_part], axis=1), jnp.stack([-sine_part, cosine], axis=1)], axis=0
    )
    inverse_lat = jnp.stack(
        [jnp.stack([cosine, -sine_part], axis=1), jnp.stack([sine_part, cosine], axis=1)], axis=0
    )
    return (
        forward_lon.astype(jnp.bfloat16),
        inverse_lon.astype(jnp.bfloat16),
        forward_lat.astype(jnp.bfloat16),
        inverse_lat.astype(jnp.bfloat16),
    )


def layer_norm(values, gain, shift):
    center = jnp.mean(values, axis=-1, keepdims=True)
    spread = jnp.mean(jnp.square(values - center), axis=-1, keepdims=True)
    return (values - center) * lax.rsqrt(spread + epsilon) * gain + shift


def soft_shrink(values):
    return values - shrink_level * jnp.tanh(values / shrink_level)


def gelu_exact(values):
    return jax.nn.gelu(values, approximate=False)


def split_blocks(spectrum):
    samples, modes_k, _, modes_m, width = spectrum.shape
    block_shape = (samples, modes_k, modes_m, BLOCKS, width // BLOCKS)
    return (spectrum[:, :, 0].reshape(block_shape), spectrum[:, :, 1].reshape(block_shape))


def join_blocks(real, imag):
    samples, modes_k, modes_m, _, _ = real.shape
    flat_shape = (samples, modes_k, modes_m, real.shape[3] * real.shape[4])
    return jnp.stack([real.reshape(flat_shape), imag.reshape(flat_shape)], axis=2)


def complex_mix(real, imag, weight, bias):
    product = partial(jnp.einsum, "skmbi,bio->skmbo", preferred_element_type=jnp.float32)
    return (
        product(real, weight[0]) - product(imag, weight[1]) + bias[0],
        product(imag, weight[0]) + product(real, weight[1]) + bias[1],
    )


def mix_back(real, imag, weight, grad_re, grad_im):
    contract = partial(jnp.einsum, "skmbi,skmbo->bio", preferred_element_type=jnp.float32)
    weight_first = contract(real, grad_re) + contract(imag, grad_im)
    weight_second = contract(real, grad_im) - contract(imag, grad_re)
    bias_grad = jnp.stack(
        [
            jnp.sum(grad_re, axis=(0, 1, 2), dtype=jnp.float32),
            jnp.sum(grad_im, axis=(0, 1, 2), dtype=jnp.float32),
        ],
        axis=0,
    )
    backward = partial(jnp.einsum, "skmbo,bio->skmbi", preferred_element_type=jnp.float32)
    input_re = backward(grad_re, weight[0]) + backward(grad_im, weight[1])
    input_im = backward(grad_im, weight[0]) - backward(grad_re, weight[1])
    return (jnp.stack([weight_first, weight_second], axis=0), bias_grad, input_re, input_im)


def shards(
    inputs,
    cotangent,
    storm_weight,
    norm_gain,
    norm_shift,
    inner_weight,
    inner_bias,
    outer_weight,
    outer_bias,
    post_gain,
    post_shift,
    expand_weight,
    expand_bias,
    reduce_weight,
    reduce_bias,
):
    slab_rows = inputs.shape[1]
    width = inputs.shape[3]
    row_ids = lax.axis_index("lat") * slab_rows + jnp.arange(slab_rows, dtype=jnp.int32)
    row_keep = (row_ids < LAT).astype(jnp.float32)
    forward_lon, inverse_lon, forward_lat, inverse_lat = make_tables()
    values = inputs.astype(jnp.float32)
    first, norm_pull = jax.vjp(layer_norm, values, norm_gain, norm_shift)
    first_low = first.astype(jnp.bfloat16)
    lon_spec = jnp.einsum(
        "srwc,wqm->srqmc", first_low, forward_lon, preferred_element_type=jnp.float32
    ).astype(jnp.bfloat16)
    mode_slab = lax.all_to_all(lon_spec, "lat", split_axis=3, concat_axis=1, tiled=True)
    freq = jnp.einsum(
        "qkpr,srpmc->skqmc", forward_lat, mode_slab, preferred_element_type=jnp.float32
    ).astype(jnp.bfloat16)
    freq_re, freq_im = split_blocks(freq)
    inner_re, inner_im = complex_mix(freq_re, freq_im, inner_weight, inner_bias)
    hidden_re_full, inner_re_pull = jax.vjp(gelu_exact, inner_re)
    hidden_im_full, inner_im_pull = jax.vjp(gelu_exact, inner_im)
    hidden_re = hidden_re_full.astype(jnp.bfloat16)
    hidden_im = hidden_im_full.astype(jnp.bfloat16)
    outer_re, outer_im = complex_mix(hidden_re, hidden_im, outer_weight, outer_bias)
    shrunk_re, outer_re_pull = jax.vjp(soft_shrink, outer_re)
    shrunk_im, outer_im_pull = jax.vjp(soft_shrink, outer_im)
    shrunk = join_blocks(shrunk_re.astype(jnp.bfloat16), shrunk_im.astype(jnp.bfloat16))
    back_slab = jnp.einsum(
        "qrpk,skpmc->srqmc", inverse_lat, shrunk, preferred_element_type=jnp.float32
    ).astype(jnp.bfloat16)
    row_spec = lax.all_to_all(back_slab, "lat", split_axis=1, concat_axis=3, tiled=True)
    filtered = jnp.einsum(
        "wqm,srqmc->srwc", inverse_lon, row_spec, preferred_element_type=jnp.float32
    )
    mixed = filtered + first + values
    second, post_pull = jax.vjp(layer_norm, mixed, post_gain, post_shift)
    second_low = second.astype(jnp.bfloat16).reshape(-1, width)
    pre_act = jnp.dot(second_low, expand_weight, preferred_element_type=jnp.float32) + expand_bias
    activ, gelu_pull = jax.vjp(gelu_exact, pre_act)
    activ_low = activ.astype(jnp.bfloat16)
    branch = jnp.dot(activ_low, reduce_weight, preferred_element_type=jnp.float32) + reduce_bias
    total = mixed + branch.reshape(mixed.shape)
    layer_out = (total * row_keep[None, :, None, None]).astype(jnp.bfloat16)
    sample_scale = storm_weight.astype(jnp.float32) / 64.0
    upstream = (
        cotangent.astype(jnp.float32)
        * sample_scale[:, None, None, None]
        * row_keep[None, :, None, None]
    )
    up_low = upstream.astype(jnp.bfloat16).reshape(-1, width)
    reduce_bias_grad = jnp.sum(up_low, axis=0, dtype=jnp.float32)
    reduce_weight_grad = jnp.dot(activ_low.T, up_low, preferred_element_type=jnp.float32)
    activ_grad = jnp.dot(up_low, reduce_weight.T, preferred_element_type=jnp.float32)
    pre_grad = gelu_pull(activ_grad)[0].astype(jnp.bfloat16)
    expand_bias_grad = jnp.sum(pre_grad, axis=0, dtype=jnp.float32)
    expand_weight_grad = jnp.dot(second_low.T, pre_grad, preferred_element_type=jnp.float32)
    second_grad = jnp.dot(pre_grad, expand_weight.T, preferred_element_type=jnp.float32).reshape(
        mixed.shape
    )
    mixed_norm_grad, post_gain_grad, post_shift_grad = post_pull(second_grad)
    mixed_grad = upstream + mixed_norm_grad
    filt_low = mixed_grad.astype(jnp.bfloat16)
    row_grad = jnp.einsum(
        "wqm,srwc->srqmc", inverse_lon, filt_low, preferred_element_type=jnp.float32
    ).astype(jnp.bfloat16)
    mode_grad = lax.all_to_all(row_grad, "lat", split_axis=3, concat_axis=1, tiled=True)
    merged_grad = jnp.einsum(
        "qrpk,srqmc->skpmc", inverse_lat, mode_grad, preferred_element_type=jnp.float32
    )
    merged_re, merged_im = split_blocks(merged_grad)
    outer_re_grad = outer_re_pull(merged_re)[0].astype(jnp.bfloat16)
    outer_im_grad = outer_im_pull(merged_im)[0].astype(jnp.bfloat16)
    outer_weight_grad, outer_bias_grad, hidden_re_grad, hidden_im_grad = mix_back(
        hidden_re, hidden_im, outer_weight, outer_re_grad, outer_im_grad
    )
    inner_re_grad = inner_re_pull(hidden_re_grad)[0].astype(jnp.bfloat16)
    inner_im_grad = inner_im_pull(hidden_im_grad)[0].astype(jnp.bfloat16)
    inner_weight_grad, inner_bias_grad, freq_re_grad, freq_im_grad = mix_back(
        freq_re, freq_im, inner_weight, inner_re_grad, inner_im_grad
    )
    freq_grad = join_blocks(freq_re_grad.astype(jnp.bfloat16), freq_im_grad.astype(jnp.bfloat16))
    slab_grad = jnp.einsum(
        "qkpr,skqmc->srpmc", forward_lat, freq_grad, preferred_element_type=jnp.float32
    ).astype(jnp.bfloat16)
    lon_grad = lax.all_to_all(slab_grad, "lat", split_axis=1, concat_axis=3, tiled=True)
    first_grad = (
        jnp.einsum("wqm,srqmc->srwc", forward_lon, lon_grad, preferred_element_type=jnp.float32)
        + mixed_grad
    )
    values_grad, norm_gain_grad, norm_shift_grad = norm_pull(first_grad)
    input_grad = values_grad + mixed_grad
    grads = (
        norm_gain_grad,
        norm_shift_grad,
        inner_weight_grad,
        inner_bias_grad,
        outer_weight_grad,
        outer_bias_grad,
        post_gain_grad,
        post_shift_grad,
        expand_weight_grad,
        expand_bias_grad,
        reduce_weight_grad,
        reduce_bias_grad,
    )
    summed = lax.psum(
        (
            grads[0],
            grads[1],
            grads[2],
            grads[3],
            grads[4],
            grads[5],
            grads[6],
            grads[7],
            grads[8],
            grads[9],
            grads[10],
            grads[11],
        ),
        ("dp", "lat"),
    )
    return (
        layer_out,
        input_grad,
        summed[0],
        summed[1],
        summed[2],
        summed[3],
        summed[4],
        summed[5],
        summed[6],
        summed[7],
        summed[8],
        summed[9],
        summed[10],
        summed[11],
    )


def solution(mesh):
    return jax.shard_map(
        shards,
        mesh=mesh,
        in_specs=(
            P("dp", "lat", None, None),
            P("dp", "lat", None, None),
            P("dp"),
            P(),
            P(),
            P(),
            P(),
            P(),
            P(),
            P(),
            P(),
            P(),
            P(),
            P(),
            P(),
        ),
        out_specs=(
            P("dp", "lat", None, None),
            P("dp", "lat", None, None),
            P(),
            P(),
            P(),
            P(),
            P(),
            P(),
            P(),
            P(),
            P(),
            P(),
            P(),
            P(),
        ),
        check_vma=False,
    )
```

profile of v0, /device:TPU:0, one launch (start us, length us, event | category | flops | bytes accessed | tf_op | source)
XLA Modules:
  0.0 1046.6 jit_solution(9826930769798211330)
XLA Ops:
  14.2 5.4 copy.128
  19.7 7.7 all-to-all-start
  31.0 75.5 %all-to-all-done = bf16[1,12,2,96,768]{4,2,1,0,3:T(2,128)(2,1)S(1)} async-done(((bf16[1,12,2,96,768]{4,2,1,0,3:T(2,128)(2,1)}), bf16[1,12,2,96,768]{4,2,1,0,3:T(2,128)(2,1)S(1)}, u32[]{:S(2)}, u32[]{:S(2)}) %all-to-all-start) | async-done | bytes 3538976 | tf_op jit(solution)/shard_map/all_to_all | solution.py:133
  121.6 5.5 reshape.763
  135.3 11.1 %fusion.115 = (bf16[96,12,8,96]{3,0,1,2:T(8,128)(2,1)S(1)}, f32[1,96,12,8,96]{4,1,2,3,0:T(8,128)}) fusion(f32[8,96,1,96,12]{1,3,4,0,2:T(8,128)S(1)} %bitcast_add_fusion.4), kind=kLoop, calls=%fused_computation.168 | loop fusion | flops 57507840 | bytes 8847360 | tf_op jit(solution)/shard_map/reshape.13
  147.4 11.1 %fusion.116 = (bf16[96,12,8,96]{3,0,1,2:T(8,128)(2,1)S(1)}, f32[1,96,12,8,96]{4,1,2,3,0:T(8,128)}) fusion(f32[8,96,1,96,12]{1,3,4,0,2:T(8,128)S(1)} %bitcast_add_fusion.3), kind=kLoop, calls=%fused_computation.169 | loop fusion | flops 57507840 | bytes 8847360 | tf_op jit(solution)/shard_map/reshape.34
  173.6 5.7 subtract_convert_fusion.1
  186.8 5.4 copy.140
  201.8 5.6 reshape.770
  208.5 67.5 %all-to-all-done.1 = bf16[1,96,2,12,768]{4,2,3,0,1:T(2,128)(2,1)} async-done(((bf16[1,96,2,12,768]{4,2,3,0,1:T(2,128)(2,1)}), bf16[1,96,2,12,768]{4,2,3,0,1:T(2,128)(2,1)}, u32[]{:S(2)}, u32[]{:S(2)}) %all-to-all-start.1) | async-done | bytes 3538976 | tf_op jit(solution)/shard_map/all_to_all | solution.py:150
  296.2 70.7 %multiply_convert_fusion = (bf16[2160,3072]{1,0:T(8,128)(2,1)}, f32[2160,3072]{1,0:T(8,128)}, f32[2160,3072]{1,0:T(8,128)}) fusion(f32[3072]{0:T(1024)S(1)} %copy-done.78, bf16[2160,768]{1,0:T(8,128)(2,1)} %reshape.768, bf16[768,3072]{1,0:T(8,128)(2,1)} %param.26), kind=kOutput, calls=%fused_computation.4 | convolution fusion | flops 10630103040 | bytes 74403840 | tf_op jit(solution)/shard_map/dot_general | solution.py:157
  366.9 29.7 %convert_reduce_fusion = (f32[3072]{0:T(1024)}, bf16[2160,3072]{1,0:T(8,128)(2,1)}) fusion(f32[2160,3072]{1,0:T(8,128)} %get-tuple-element.97, bf16[2160,768]{1,0:T(8,128)(2,1)S(1)} %copy-done.27, bf16[3072,768]{1,0:T(8,128)(2,1)} %param.28, f32[2160,3072]{1,0:T(8,128)} %get-tuple-element.131, f32[3072]{0:T(1024)S(1)} %copy-done.78), kind=kOutput, calls=%fused_computation.2 | convolution fusion | flops 10304959488 | bytes 74416128 | tf_op jit(solution)/shard_map/dot_general | solution.py:172
  396.6 16.6 %fusion.285 = (f32[768]{0:T(1024)}, f32[2160]{0:T(1024)S(1)}, f32[2160,768]{1,0:T(8,128)}) fusion(f32[2160]{0:T(1024)S(1)} %copy-done.69, f32[768]{0:T(1024)S(1)} %copy-done.59, bf16[2160,3072]{1,0:T(8,128)(2,1)} %get-tuple-element.139, bf16[768,3072]{1,0:T(8,128)(2,1)S(1)} %copy-done.77), kind=kOutput, calls=%fused_computation.331 | convolution fusion | flops 10198791168 | bytes 24648576 | tf_op jit(solution)/shard_map/dot_general | solution.py:176
  413.2 7.3 reshape.771
  420.5 7.6 multiply_reduce_fusion
  429.7 16.7 %convolution_add_fusion = f32[2160,768]{1,0:T(8,128)} fusion(bf16[2160,3072]{1,0:T(8,128)(2,1)} %get-tuple-element.96, bf16[3072,768]{1,0:T(8,128)(2,1)} %param.28, f32[768]{0:T(1024)S(1)} %copy-done.79), kind=kOutput, calls=%fused_computation.55 | convolution fusion | flops 10193817600 | bytes 24628224 | tf_op jit(solution)/shard_map/dot_general | solution.py:160
  446.4 7.5 reshape.769
  453.9 9.9 add_add_fusion
  467.9 5.4 copy.143
  477.0 17.8 %fusion.293 = f32[768,3072]{1,0:T(8,128)} fusion(bf16[2160,768]{1,0:T(8,128)(2,1)} %reshape.768, bf16[2160,3072]{1,0:T(8,128)(2,1)} %get-tuple-element.139), kind=kOutput, calls=%fused_computation.335 | convolution fusion | flops 10192158720 | bytes 26025984 | tf_op jit(solution)/shard_map/dot_general | solution.py:175
  494.8 16.9 %fusion.294 = f32[3072,768]{1,0:T(8,128)} fusion(bf16[2160,3072]{1,0:T(8,128)(2,1)} %get-tuple-element.96, bf16[2160,768]{1,0:T(8,128)(2,1)S(1)} %copy-done.28), kind=kOutput, calls=%fused_computation.336 | convolution fusion | flops 10192158720 | bytes 26025984 | tf_op jit(solution)/shard_map/dot_general | solution.py:171
  511.7 44.5 %all-to-all-done.2 = bf16[1,12,2,96,768]{4,2,1,0,3:T(2,128)(2,1)S(1)} async-done(((bf16[1,12,2,96,768]{4,2,1,0,3:T(2,128)(2,1)}), bf16[1,12,2,96,768]{4,2,1,0,3:T(2,128)(2,1)S(1)}, u32[]{:S(2)}, u32[]{:S(2)}) %all-to-all-start.2) | async-done | bytes 3538976 | tf_op jit(solution)/shard_map/all_to_all | solution.py:185
  577.3 5.7 reshape_squeeze.9
  582.9 5.5 convert_reduce_fusion.3
  604.3 5.5 convert_reduce_fusion.5
  633.2 5.4 copy.157
  643.2 117.1 %all-to-all-done.3 = bf16[1,96,2,12,768]{4,2,3,0,1:T(2,128)(2,1)} async-done(((bf16[1,96,2,12,768]{4,2,3,0,1:T(2,128)(2,1)}), bf16[1,96,2,12,768]{4,2,3,0,1:T(2,128)(2,1)}, u32[]{:S(2)}, u32[]{:S(2)}) %all-to-all-start.3) | async-done | bytes 3538976 | tf_op jit(solution)/shard_map/all_to_all | solution.py:204
  765.5 7.1 fusion.19
  776.5 8.1 copy.168
  784.7 41.8 %all-reduce = (f32[768]{0:T(1024)}, f32[768]{0:T(1024)}, f32[2,8,96]{2,1,0:T(8,128)}, f32[2,8,96]{2,1,0:T(8,128)}, f32[768]{0:T(1024)}, /*index=5*/f32[768]{0:T(1024)}, f32[3072]{0:T(1024)}, f32[768]{0:T(1024)}) all-reduce(f32[768]{0:T(1024)S(1)} %get-tuple-element.72, ...), channel_id=1, replica_groups=mesh['dp'=4,'lat'=8] {'dp','lat'}, use_global_device_ids=true, to_apply=%region_11.12 | all-reduce | flops 9984 | bytes 79872 | tf_op jit(solution)/shard_map/psum | solution.py:225
  826.4 196.3 %all-reduce.4.cloned.1.call-done = (f32[2,8,96,96]{3,2,1,0:T(8,128)}, f32[2,8,96,96]{3,2,1,0:T(8,128)}, f32[768,3072]{1,0:T(8,128)}, f32[3072,768]{1,0:T(8,128)}) async-done(((f32[2,8,96,96]{3,2,1,0:T(8,128)}, f32[2,8,96,96]{3,2,1,0:T(8,128)}, f32[768,3072]{1,0:T(8,128)}, f32[3072,768]{1,0:T(8,128)}), (f32[2,8,96,96]{3,2,1,0:T(8,128)}, f32[2,8,96,96]{3,2,1,0:T(8,128)}, f32[768,3072]{1,0:T(8,128)}, ...) | async-done | bytes 20054032 | tf_op jit(solution)/shard_map/psum | solution.py:225
  1027.0 8.8 copy.240
  (277 shorter events, 177.8 us)
Async XLA Ops:
  10.2 270.9 %copy-start.33 = (f32[12,180]{1,0:T(8,128)}, f32[12,180]{1,0:T(8,128)S(1)}, u32[]{:S(2)}) copy-start(f32[12,180]{1,0:T(8,128)S(1)} %broadcast_multiply_fusion.1) | copy-start | bytes 25924
  19.7 86.8 %all-to-all-start = ((bf16[1,12,2,96,768]{4,2,1,0,3:T(2,128)(2,1)}), bf16[1,12,2,96,768]{4,2,1,0,3:T(2,128)(2,1)S(1)}, u32[]{:S(2)}, u32[]{:S(2)}) async-start(bf16[1,12,2,96,768]{4,2,1,0,3:T(2,128)(2,1)} %copy.128), calls=%async_computation | async-start | bytes 7077888 | tf_op jit(solution)/shard_map/all_to_all | solution.py:133
  121.5 24.9 %copy-start.1 = (bf16[96,12,8,96]{0,3,1,2:T(8,128)(2,1)}, bf16[96,12,8,96]{0,3,1,2:T(8,128)(2,1)S(1)}, u32[]{:S(2)}) copy-start(bf16[96,12,8,96]{0,3,1,2:T(8,128)(2,1)S(1)} %copy.160) | copy-start | bytes 5308420
  135.3 11.1 %copy-start.20 = (f32[8,96,1,96,12]{1,3,4,0,2:T(8,128)}, f32[8,96,1,96,12]{1,3,4,0,2:T(8,128)S(1)}, u32[]{:S(2)}) copy-start(f32[8,96,1,96,12]{1,3,4,0,2:T(8,128)S(1)} %bitcast_add_fusion.4) | copy-start | bytes 10616836
  135.3 11.1 %copy-start.62 = (f32[8,96]{1,0:T(8,128)S(1)}, f32[8,96]{1,0:T(8,128)}, u32[]{:S(2)}) copy-start(f32[8,96]{1,0:T(8,128)} %get-tuple-element.117) | copy-start | bytes 9220
  146.4 12.1 %copy-start.11 = (bf16[96,12,8,96]{3,0,1,2:T(8,128)(2,1)}, bf16[96,12,8,96]{3,0,1,2:T(8,128)(2,1)S(1)}, u32[]{:S(2)}) copy-start(bf16[96,12,8,96]{3,0,1,2:T(8,128)(2,1)S(1)} %get-tuple-element.98) | copy-start | bytes 5308420
  147.4 11.1 %copy-start.19 = (f32[8,96,1,96,12]{1,3,4,0,2:T(8,128)}, f32[8,96,1,96,12]{1,3,4,0,2:T(8,128)S(1)}, u32[]{:S(2)}) copy-start(f32[8,96,1,96,12]{1,3,4,0,2:T(8,128)S(1)} %bitcast_add_fusion.3) | copy-start | bytes 10616836
  147.4 11.1 %copy-start.25 = (bf16[2,8,96,96]{3,2,1,0:T(8,128)(2,1)S(1)}, bf16[2,8,96,96]{3,2,1,0:T(8,128)(2,1)}, u32[]{:S(2)}) copy-start(bf16[2,8,96,96]{3,2,1,0:T(8,128)(2,1)} %param.22) | copy-start | bytes 884740
  192.3 83.7 %all-to-all-start.1 = ((bf16[1,96,2,12,768]{4,2,3,0,1:T(2,128)(2,1)}), bf16[1,96,2,12,768]{4,2,3,0,1:T(2,128)(2,1)}, u32[]{:S(2)}, u32[]{:S(2)}) async-start(bf16[1,96,2,12,768]{4,2,3,0,1:T(2,128)(2,1)} %copy.140), calls=%async_computation.1 | async-start | bytes 7077888 | tf_op jit(solution)/shard_map/all_to_all | solution.py:150
  207.4 73.7 %copy-start.6 = (bf16[1,12,180,768]{3,2,1,0:T(8,128)(2,1)S(1)}, bf16[1,12,180,768]{3,2,1,0:T(8,128)(2,1)}, u32[]{:S(2)}) copy-start(bf16[1,12,180,768]{3,2,1,0:T(8,128)(2,1)} %param.15) | copy-start | bytes 9953284
  207.4 73.7 %copy-start.56 = (f32[12,180]{1,0:T(8,128)S(1)}, f32[12,180]{1,0:T(8,128)}, u32[]{:S(2)}) copy-start(f32[12,180]{1,0:T(8,128)} %copy-done.55) | copy-start | bytes 25924
  207.4 73.7 %copy-start.65 = (f32[768]{0:T(1024)S(1)}, f32[768]{0:T(1024)}, u32[]{:S(2)}) copy-start(f32[768]{0:T(1024)} %param.18) | copy-start | bytes 9220
  207.4 73.7 %copy-start.72 = (f32[768]{0:T(1024)S(1)}, f32[768]{0:T(1024)}, u32[]{:S(2)}) copy-start(f32[768]{0:T(1024)} %param.19) | copy-start | bytes 9220
  208.5 75.8 %copy-start.39 = (f32[180,1,96]{2,0,1:T(8,128)}, f32[180,1,96]{2,0,1:T(8,128)S(1)}, u32[]{:S(2)}) copy-start(f32[180,1,96]{2,0,1:T(8,128)S(1)} %get-tuple-element.118) | copy-start | bytes 207364
  296.2 70.7 %copy-start.27 = (bf16[2160,768]{1,0:T(8,128)(2,1)S(1)}, bf16[2160,768]{1,0:T(8,128)(2,1)}, u32[]{:S(2)}) copy-start(bf16[2160,768]{1,0:T(8,128)(2,1)} %reshape.770) | copy-start | bytes 9953284
  366.9 29.7 %copy-start.59 = (f32[768]{0:T(1024)S(1)}, f32[768]{0:T(1024)}, u32[]{:S(2)}) copy-start(f32[768]{0:T(1024)} %param.24) | copy-start | bytes 9220
  366.9 29.7 %copy-start.69 = (f32[2160]{0:T(1024)S(1)}, f32[2160]{0:T(1024)}, u32[]{:S(2)}) copy-start(f32[2160]{0:T(1024)} %rsqrt.26) | copy-start | bytes 25924
  366.9 29.7 %copy-start.77 = (bf16[768,3072]{1,0:T(8,128)(2,1)S(1)}, bf16[768,3072]{1,0:T(8,128)(2,1)}, u32[]{:S(2)}) copy-start(bf16[768,3072]{1,0:T(8,128)(2,1)} %param.26) | copy-start | bytes 14155780
  413.2 15.0 %slice-start = ((s8[6782976]{0:T(1024)(128)(4,1)}), s8[2588672]{0:T(1024)(128)(4,1)S(1)}, s32[]{:S(2)}) async-start(s8[6782976]{0:T(1024)(128)(4,1)} %bitcast.614), calls=%async_computation.5 | async-start | bytes 5177344
  453.9 12.7 %copy-start.40 = (f32[180,1,96]{2,0,1:T(8,128)S(1)}, f32[180,1,96]{2,0,1:T(8,128)}, u32[]{:S(2)}) copy-start(f32[180,1,96]{2,0,1:T(8,128)} %copy-done.39) | copy-start | bytes 207364
  453.9 12.7 %copy-start.42 = (f32[180,1,96]{2,0,1:T(8,128)S(1)}, f32[180,1,96]{2,0,1:T(8,128)}, u32[]{:S(2)}) copy-start(f32[180,1,96]{2,0,1:T(8,128)} %get-tuple-element.119) | copy-start | bytes 207364
  473.3 82.9 %all-to-all-start.2 = ((bf16[1,12,2,96,768]{4,2,1,0,3:T(2,128)(2,1)}), bf16[1,12,2,96,768]{4,2,1,0,3:T(2,128)(2,1)S(1)}, u32[]{:S(2)}, u32[]{:S(2)}) async-start(bf16[1,12,2,96,768]{4,2,1,0,3:T(2,128)(2,1)} %copy.143), calls=%async_computation.2 | async-start | bytes 7077888 | tf_op jit(solution)/shard_map/all_to_all | solution.py:185
  477.0 545.8 %all-reduce.4.cloned.1.call-start = ((), (), s32[]{:S(2)}) async-start(), calls=%async_computation.4 | async-start | bytes 40894464 | tf_op jit(solution)/shard_map/psum | solution.py:225
  477.0 17.8 %copy-start.28 = (bf16[2160,768]{1,0:T(8,128)(2,1)S(1)}, bf16[2160,768]{1,0:T(8,128)(2,1)}, u32[]{:S(2)}) copy-start(bf16[2160,768]{1,0:T(8,128)(2,1)} %reshape.770) | copy-start | bytes 9953284
  596.9 15.2 %copy-start.8 = (bf16[1,96,12,8,96]{4,1,2,3,0:T(8,128)(2,1)}, bf16[1,96,12,8,96]{4,1,2,3,0:T(8,128)(2,1)S(1)}, u32[]{:S(2)}) copy-start(bf16[1,96,12,8,96]{4,1,2,3,0:T(8,128)(2,1)S(1)} %get-tuple-element.137) | copy-start | bytes 5308420
  638.7 121.7 %all-to-all-start.3 = ((bf16[1,96,2,12,768]{4,2,3,0,1:T(2,128)(2,1)}), bf16[1,96,2,12,768]{4,2,3,0,1:T(2,128)(2,1)}, u32[]{:S(2)}, u32[]{:S(2)}) async-start(bf16[1,96,2,12,768]{4,2,3,0,1:T(2,128)(2,1)} %copy.157), calls=%async_computation.3 | async-start | bytes 7077888 | tf_op jit(solution)/shard_map/all_to_all | solution.py:204
  643.2 122.3 %copy-start.7 = (bf16[1,12,180,768]{3,2,1,0:T(8,128)(2,1)S(1)}, bf16[1,12,180,768]{3,2,1,0:T(8,128)(2,1)}, u32[]{:S(2)}) copy-start(bf16[1,12,180,768]{3,2,1,0:T(8,128)(2,1)} %param.15) | copy-start | bytes 9953284
  643.2 122.3 %copy-start.34 = (f32[12,180]{1,0:T(8,128)S(1)}, f32[12,180]{1,0:T(8,128)}, u32[]{:S(2)}) copy-start(f32[12,180]{1,0:T(8,128)} %copy-done.33) | copy-start | bytes 25924
  643.2 122.3 %copy-start.36 = (f32[180,1,96]{2,0,1:T(8,128)S(1)}, f32[180,1,96]{2,0,1:T(8,128)}, u32[]{:S(2)}) copy-start(f32[180,1,96]{2,0,1:T(8,128)} %copy-done.35) | copy-start | bytes 207364
  643.2 122.3 %copy-start.57 = (f32[12,180]{1,0:T(8,128)S(1)}, f32[12,180]{1,0:T(8,128)}, u32[]{:S(2)}) copy-start(f32[12,180]{1,0:T(8,128)} %copy-done.55) | copy-start | bytes 25924
  643.2 122.3 %copy-start.66 = (f32[768]{0:T(1024)S(1)}, f32[768]{0:T(1024)}, u32[]{:S(2)}) copy-start(f32[768]{0:T(1024)} %param.18) | copy-start | bytes 9220
  1024.8 11.0 %slice-start.8 = ((s8[9437184]{0:T(1024)(128)(4,1)}), s8[4194304]{0:T(1024)(128)(4,1)S(1)}, s32[]{:S(2)}) async-start(s8[9437184]{0:T(1024)(128)(4,1)} %bitcast.626), calls=%async_computation.13 | async-start | bytes 8388608
  (64 other events, 319.8 us)
Sparse Core Ops, SparseCore 0:
  623.1 399.6 all-reduce.3
where the time goes:
time: 1050 us
  waiting for transfers between devices  501 us (48%)
  matrix products  232 us (22%)
  local copies, waits for them, and re-layouts  162 us (15%)
  other arithmetic  72.2 us (7%)
  blocking collectives  41.8 us (4%)
  starting transfers between devices  21.1 us (2%)
  between operations  16.2 us (2%)
    psum x1, waiting for transfers between devices, shards(): lax.psum((grads[0], grads[1], grads[2], grads[3], grads[4], grads[5], gra...  196 us
    all_to_all x1, waiting for transfers between devices, shards(): lax.all_to_all(slab_grad, 'lat', split_axis=1, concat_axis=3, tiled=True)  117 us
    all_to_all x1, waiting for transfers between devices, shards(): lax.all_to_all(lon_spec, 'lat', split_axis=3, concat_axis=1, tiled=True)  75.5 us
    dot_general x1, matrix products, shards(): jnp.dot(second_low, expand_weight, preferred_element_type=jnp.float32)  70.7 us
    all_to_all x1, waiting for transfers between devices, shards(): lax.all_to_all(back_slab, 'lat', split_axis=1, concat_axis=3, tiled=True)  67.5 us
    all_to_all x1, waiting for transfers between devices, shards(): lax.all_to_all(row_grad, 'lat', split_axis=3, concat_axis=1, tiled=True)  44.5 us
    psum x1, blocking collectives, shards(): lax.psum((grads[0], grads[1], grads[2], grads[3], grads[4], grads[5], gra...  41.8 us
    unnamed x187, local copies, waits for them, and re-layouts  37.9 us
  transfers between devices with their start and end apart: 5, of which 5 were waited for; matrix products, arithmetic and copies ran while one was open for 8% of the time, Pallas kernels for 0%

commit v1 on v0

--- a/solution.py
+++ b/solution.py
@@ -222,23 +222,22 @@
         reduce_weight_grad,
         reduce_bias_grad,
     )
-    summed = lax.psum(
-        (
-            grads[0],
-            grads[1],
-            grads[2],
-            grads[3],
-            grads[4],
-            grads[5],
-            grads[6],
-            grads[7],
-            grads[8],
-            grads[9],
-            grads[10],
-            grads[11],
-        ),
-        ("dp", "lat"),
-    )
+    summed = (
+        grads[0],
+        grads[1],
+        grads[2],
+        grads[3],
+        grads[4],
+        grads[5],
+        grads[6],
+        grads[7],
+        grads[8],
+        grads[9],
+        grads[10],
+        grads[11],
+    )
+    for mesh_axis in ("lat", "dp"):
+        summed = lax.psum(summed, mesh_axis)
     return (
         layer_out,
         input_grad,

time: 1050 us -> 1610 us (1.53)
  waiting for transfers between devices: 501 us -> 1050 us
    psum x1 -> x2, waiting for transfers between devices: 196 us -> 779 us  [shards(): summed = lax.psum(summed, mesh_axis)]
    all_to_all x1, waiting for transfers between devices: 117 us -> 79.7 us  [shards(): lax.all_to_all(slab_grad, 'lat', split_axis=1, concat_axis=3, tiled=True)]
    psum x1 -> x2, blocking collectives: 41.8 us -> 49.3 us  [shards(): summed = lax.psum(summed, mesh_axis)]
    unnamed x187 -> x189, local copies, waits for them, and re-layouts: 37.9 us -> 39.4 us
  transfers between devices with their start and end apart: 5 -> 6, of which waited for: 5 -> 6; matrix products, arithmetic and copies ran while one was open for 8% -> 6% of each run, Pallas kernels for 0% -> 0%
where the time goes in v1:
time: 1610 us; the launch traced here: 1600 us
  waiting for transfers between devices  1050 us (65%)
  matrix products  234 us (15%)
  local copies, waits for them, and re-layouts  163 us (10%)
  other arithmetic  70.9 us (4%)
  blocking collectives  49.3 us (3%)
  starting transfers between devices  21.5 us (1%)
  between operations  16.3 us (1%)
    psum x2, waiting for transfers between devices, shards(): summed = lax.psum(summed, mesh_axis)  779 us
    all_to_all x1, waiting for transfers between devices, shards(): lax.all_to_all(slab_grad, 'lat', split_axis=1, concat_axis=3, tiled=True)  79.7 us
    all_to_all x1, waiting for transfers between devices, shards(): lax.all_to_all(lon_spec, 'lat', split_axis=3, concat_axis=1, tiled=True)  75.5 us
    dot_general x1, matrix products, shards(): jnp.dot(second_low, expand_weight, preferred_element_type=jnp.float32)  70.3 us
    all_to_all x1, waiting for transfers between devices, shards(): lax.all_to_all(back_slab, 'lat', split_axis=1, concat_axis=3, tiled=True)  67.5 us
    psum x2, blocking collectives, shards(): summed = lax.psum(summed, mesh_axis)  49.3 us
    all_to_all x1, waiting for transfers between devices, shards(): lax.all_to_all(row_grad, 'lat', split_axis=3, concat_axis=1, tiled=True)  44.4 us
    unnamed x189, local copies, waits for them, and re-layouts  39.4 us
  transfers between devices with their start and end apart: 6, of which 6 were waited for; matrix products, arithmetic and copies ran while one was open for 6% of the time, Pallas kernels for 0%

profile of v1, /device:TPU:0, one launch (start us, length us, event | category | flops | bytes accessed | tf_op | source)
XLA Modules:
  0.0 1601.7 jit_solution(8874353259919118157)
XLA Ops:
  14.2 5.4 copy.128
  19.6 7.7 all-to-all-start
  31.0 75.5 %all-to-all-done = bf16[1,12,2,96,768]{4,2,1,0,3:T(2,128)(2,1)S(1)} async-done(((bf16[1,12,2,96,768]{4,2,1,0,3:T(2,128)(2,1)}), bf16[1,12,2,96,768]{4,2,1,0,3:T(2,128)(2,1)S(1)}, u32[]{:S(2)}, u32[]{:S(2)}) %all-to-all-start) | async-done | bytes 3538976 | tf_op jit(solution)/shard_map/all_to_all | solution.py:133
  121.6 5.5 reshape.763
  135.3 11.1 fusion.115
  147.4 11.1 fusion.116
  173.5 5.7 subtract_convert_fusion.1
  186.8 5.4 copy.140
  201.8 5.6 reshape.770
  208.5 67.5 %all-to-all-done.1 = bf16[1,96,2,12,768]{4,2,3,0,1:T(2,128)(2,1)} async-done(((bf16[1,96,2,12,768]{4,2,3,0,1:T(2,128)(2,1)}), bf16[1,96,2,12,768]{4,2,3,0,1:T(2,128)(2,1)}, u32[]{:S(2)}, u32[]{:S(2)}) %all-to-all-start.1) | async-done | bytes 3538976 | tf_op jit(solution)/shard_map/all_to_all | solution.py:150
  296.1 70.3 %multiply_convert_fusion = (bf16[2160,3072]{1,0:T(8,128)(2,1)}, f32[2160,3072]{1,0:T(8,128)}, f32[2160,3072]{1,0:T(8,128)}) fusion(f32[3072]{0:T(1024)S(1)} %copy-done.79, bf16[2160,768]{1,0:T(8,128)(2,1)} %reshape.768, bf16[768,3072]{1,0:T(8,128)(2,1)} %param.26), kind=kOutput, calls=%fused_computation.4 | convolution fusion | flops 10630103040 | bytes 74403840 | tf_op jit(solution)/shard_map/dot_general | solution.py:157
  366.5 29.7 %convert_reduce_fusion = (f32[3072]{0:T(1024)}, bf16[2160,3072]{1,0:T(8,128)(2,1)}) fusion(f32[2160,3072]{1,0:T(8,128)} %get-tuple-element.109, bf16[2160,768]{1,0:T(8,128)(2,1)S(1)} %copy-done.28, bf16[3072,768]{1,0:T(8,128)(2,1)} %param.28, f32[2160,3072]{1,0:T(8,128)} %get-tuple-element.143, f32[3072]{0:T(1024)S(1)} %copy-done.79), kind=kOutput, calls=%fused_computation.2 | convolution fusion | flops 10304959488 | bytes 74416128 | tf_op jit(solution)/shard_map/dot_general | solution.py:172
  396.2 16.6 %fusion.285 = (f32[768]{0:T(1024)}, f32[2160]{0:T(1024)S(1)}, f32[2160,768]{1,0:T(8,128)}) fusion(f32[2160]{0:T(1024)S(1)} %copy-done.70, f32[768]{0:T(1024)S(1)} %copy-done.60, bf16[2160,3072]{1,0:T(8,128)(2,1)} %get-tuple-element.151, bf16[768,3072]{1,0:T(8,128)(2,1)S(1)} %copy-done.78), kind=kOutput, calls=%fused_computation.331 | convolution fusion | flops 10198791168 | bytes 24648576 | tf_op jit(solution)/shard_map/dot_general | solution.py:176
  412.8 7.3 reshape.771
  420.1 7.4 multiply_reduce_fusion
  429.0 16.7 %convolution_add_fusion = f32[2160,768]{1,0:T(8,128)} fusion(bf16[2160,3072]{1,0:T(8,128)(2,1)} %get-tuple-element.108, bf16[3072,768]{1,0:T(8,128)(2,1)} %param.28, f32[768]{0:T(1024)S(1)} %copy-done.80), kind=kOutput, calls=%fused_computation.55 | convolution fusion | flops 10193817600 | bytes 24628224 | tf_op jit(solution)/shard_map/dot_general | solution.py:160
  445.7 7.5 reshape.769
  453.2 9.9 add_add_fusion
  467.1 5.4 copy.143
  476.3 17.9 %fusion.293 = f32[768,3072]{1,0:T(8,128)} fusion(bf16[2160,768]{1,0:T(8,128)(2,1)} %reshape.768, bf16[2160,3072]{1,0:T(8,128)(2,1)} %get-tuple-element.151), kind=kOutput, calls=%fused_computation.335 | convolution fusion | flops 10192158720 | bytes 26025984 | tf_op jit(solution)/shard_map/dot_general | solution.py:175
  494.2 16.9 %fusion.294 = f32[3072,768]{1,0:T(8,128)} fusion(bf16[2160,3072]{1,0:T(8,128)(2,1)} %get-tuple-element.108, bf16[2160,768]{1,0:T(8,128)(2,1)S(1)} %copy-done.29), kind=kOutput, calls=%fused_computation.336 | convolution fusion | flops 10192158720 | bytes 26025984 | tf_op jit(solution)/shard_map/dot_general | solution.py:171
  511.1 44.4 %all-to-all-done.2 = bf16[1,12,2,96,768]{4,2,1,0,3:T(2,128)(2,1)S(1)} async-done(((bf16[1,12,2,96,768]{4,2,1,0,3:T(2,128)(2,1)}), bf16[1,12,2,96,768]{4,2,1,0,3:T(2,128)(2,1)S(1)}, u32[]{:S(2)}, u32[]{:S(2)}) %all-to-all-start.2) | async-done | bytes 3538976 | tf_op jit(solution)/shard_map/all_to_all | solution.py:185
  576.5 5.7 reshape_squeeze.9
  582.2 5.5 convert_reduce_fusion.3
  624.0 602.3 %all-reduce.7.cloned.1.call-done = (f32[2,8,96,96]{3,2,1,0:T(8,128)}, f32[2,8,96,96]{3,2,1,0:T(8,128)}, f32[768,3072]{1,0:T(8,128)}, f32[3072,768]{1,0:T(8,128)}) async-done(((f32[2,8,96,96]{3,2,1,0:T(8,128)}, f32[2,8,96,96]{3,2,1,0:T(8,128)}, f32[768,3072]{1,0:T(8,128)}, f32[3072,768]{1,0:T(8,128)}), (f32[2,8,96,96]{3,2,1,0:T(8,128)}, f32[2,8,96,96]{3,2,1,0:T(8,128)}, f32[768,3072]{1,0:T(8,128)}, ...) | async-done | bytes 20054032 | tf_op jit(solution)/shard_map/psum | solution.py:240
  1247.3 79.7 %all-to-all-done.3 = bf16[1,96,2,12,768]{4,2,3,0,1:T(2,128)(2,1)} async-done(((bf16[1,96,2,12,768]{4,2,3,0,1:T(2,128)(2,1)}), bf16[1,96,2,12,768]{4,2,3,0,1:T(2,128)(2,1)}, u32[]{:S(2)}, u32[]{:S(2)}) %all-to-all-start.3) | async-done | bytes 3538976 | tf_op jit(solution)/shard_map/all_to_all | solution.py:204
  1332.1 7.3 fusion.19
  1343.3 8.1 copy.168
  1351.5 35.8 %all-reduce = (f32[768]{0:T(1024)S(1)}, f32[768]{0:T(1024)S(1)}, f32[2,8,96]{2,1,0:T(8,128)S(1)}, f32[2,8,96]{2,1,0:T(8,128)S(1)}, f32[768]{0:T(1024)S(1)}, /*in...) all-reduce(f32[768]{0:T(1024)S(1)} %get-tuple-element.72, ...), channel_id=1, replica_groups=mesh['dp'=4,'lat'=8] {'lat'}, use_global_device_ids=true, to_apply=%region_11.12 | all-reduce | flops 9984 | bytes 79872 | tf_op jit(solution)/shard_map/psum | solution.py:240
  1387.3 13.5 all-reduce.2
  1400.8 177.0 %all-reduce.9.cloned.1.call-done = (f32[2,8,96,96]{3,2,1,0:T(8,128)}, f32[2,8,96,96]{3,2,1,0:T(8,128)}, f32[768,3072]{1,0:T(8,128)}, f32[3072,768]{1,0:T(8,128)}) async-done(((f32[2,8,96,96]{3,2,1,0:T(8,128)}, f32[2,8,96,96]{3,2,1,0:T(8,128)}, f32[768,3072]{1,0:T(8,128)}, f32[3072,768]{1,0:T(8,128)}), (f32[2,8,96,96]{3,2,1,0:T(8,128)}, f32[2,8,96,96]{3,2,1,0:T(8,128)}, f32[768,3072]{1,0:T(8,128)}, ...) | async-done | bytes 20054032 | tf_op jit(solution)/shard_map/psum | solution.py:240
  1582.1 8.8 copy.244
  (283 shorter events, 191.1 us)
Async XLA Ops:
  10.2 270.9 %copy-start.34 = (f32[12,180]{1,0:T(8,128)}, f32[12,180]{1,0:T(8,128)S(1)}, u32[]{:S(2)}) copy-start(f32[12,180]{1,0:T(8,128)S(1)} %broadcast_multiply_fusion.1) | copy-start | bytes 25924
  19.6 86.8 %all-to-all-start = ((bf16[1,12,2,96,768]{4,2,1,0,3:T(2,128)(2,1)}), bf16[1,12,2,96,768]{4,2,1,0,3:T(2,128)(2,1)S(1)}, u32[]{:S(2)}, u32[]{:S(2)}) async-start(bf16[1,12,2,96,768]{4,2,1,0,3:T(2,128)(2,1)} %copy.128), calls=%async_computation | async-start | bytes 7077888 | tf_op jit(solution)/shard_map/all_to_all | solution.py:133
  121.5 24.9 %copy-start.1 = (bf16[96,12,8,96]{0,3,1,2:T(8,128)(2,1)}, bf16[96,12,8,96]{0,3,1,2:T(8,128)(2,1)S(1)}, u32[]{:S(2)}) copy-start(bf16[96,12,8,96]{0,3,1,2:T(8,128)(2,1)S(1)} %copy.160) | copy-start | bytes 5308420
  135.3 11.1 copy-start.21
  135.3 11.1 copy-start.63
  146.4 12.1 copy-start.12
  147.4 11.1 copy-start.20
  147.4 11.1 copy-start.26
  192.2 83.8 %all-to-all-start.1 = ((bf16[1,96,2,12,768]{4,2,3,0,1:T(2,128)(2,1)}), bf16[1,96,2,12,768]{4,2,3,0,1:T(2,128)(2,1)}, u32[]{:S(2)}, u32[]{:S(2)}) async-start(bf16[1,96,2,12,768]{4,2,3,0,1:T(2,128)(2,1)} %copy.140), calls=%async_computation.1 | async-start | bytes 7077888 | tf_op jit(solution)/shard_map/all_to_all | solution.py:150
  207.3 73.7 %copy-start.6 = (bf16[1,12,180,768]{3,2,1,0:T(8,128)(2,1)S(1)}, bf16[1,12,180,768]{3,2,1,0:T(8,128)(2,1)}, u32[]{:S(2)}) copy-start(bf16[1,12,180,768]{3,2,1,0:T(8,128)(2,1)} %param.15) | copy-start | bytes 9953284
  207.4 73.7 %copy-start.57 = (f32[12,180]{1,0:T(8,128)S(1)}, f32[12,180]{1,0:T(8,128)}, u32[]{:S(2)}) copy-start(f32[12,180]{1,0:T(8,128)} %copy-done.56) | copy-start | bytes 25924
  207.4 73.7 %copy-start.66 = (f32[768]{0:T(1024)S(1)}, f32[768]{0:T(1024)}, u32[]{:S(2)}) copy-start(f32[768]{0:T(1024)} %param.18) | copy-start | bytes 9220
  207.4 73.7 %copy-start.73 = (f32[768]{0:T(1024)S(1)}, f32[768]{0:T(1024)}, u32[]{:S(2)}) copy-start(f32[768]{0:T(1024)} %param.19) | copy-start | bytes 9220
  208.5 75.8 %copy-start.40 = (f32[180,1,96]{2,0,1:T(8,128)}, f32[180,1,96]{2,0,1:T(8,128)S(1)}, u32[]{:S(2)}) copy-start(f32[180,1,96]{2,0,1:T(8,128)S(1)} %get-tuple-element.130) | copy-start | bytes 207364
  296.1 70.3 %copy-start.28 = (bf16[2160,768]{1,0:T(8,128)(2,1)S(1)}, bf16[2160,768]{1,0:T(8,128)(2,1)}, u32[]{:S(2)}) copy-start(bf16[2160,768]{1,0:T(8,128)(2,1)} %reshape.770) | copy-start | bytes 9953284
  366.4 29.7 %copy-start.60 = (f32[768]{0:T(1024)S(1)}, f32[768]{0:T(1024)}, u32[]{:S(2)}) copy-start(f32[768]{0:T(1024)} %param.24) | copy-start | bytes 9220
  366.4 29.7 %copy-start.70 = (f32[2160]{0:T(1024)S(1)}, f32[2160]{0:T(1024)}, u32[]{:S(2)}) copy-start(f32[2160]{0:T(1024)} %rsqrt.26) | copy-start | bytes 25924
  366.5 29.7 %copy-start.78 = (bf16[768,3072]{1,0:T(8,128)(2,1)S(1)}, bf16[768,3072]{1,0:T(8,128)(2,1)}, u32[]{:S(2)}) copy-start(bf16[768,3072]{1,0:T(8,128)(2,1)} %param.26) | copy-start | bytes 14155780
  412.8 14.7 slice-start
  453.2 12.7 copy-start.41
  453.2 12.6 copy-start.43
  472.5 82.9 %all-to-all-start.2 = ((bf16[1,12,2,96,768]{4,2,1,0,3:T(2,128)(2,1)}), bf16[1,12,2,96,768]{4,2,1,0,3:T(2,128)(2,1)S(1)}, u32[]{:S(2)}, u32[]{:S(2)}) async-start(bf16[1,12,2,96,768]{4,2,1,0,3:T(2,128)(2,1)} %copy.143), calls=%async_computation.2 | async-start | bytes 7077888 | tf_op jit(solution)/shard_map/all_to_all | solution.py:185
  476.2 750.1 %all-reduce.7.cloned.1.call-start = ((), (), s32[]{:S(2)}) async-start(), calls=%async_computation.4 | async-start | bytes 40894464 | tf_op jit(solution)/shard_map/psum | solution.py:240
  476.3 17.9 %copy-start.29 = (bf16[2160,768]{1,0:T(8,128)(2,1)S(1)}, bf16[2160,768]{1,0:T(8,128)(2,1)}, u32[]{:S(2)}) copy-start(bf16[2160,768]{1,0:T(8,128)(2,1)} %reshape.770) | copy-start | bytes 9953284
  582.2 11.3 slice-start.6
  612.9 964.9 %all-reduce.9.cloned.1.call-start = ((), (), s32[]{:S(2)}) async-start(), calls=%async_computation.5 | async-start | bytes 40894464 | tf_op jit(solution)/shard_map/psum | solution.py:240
  1242.5 84.5 %all-to-all-start.3 = ((bf16[1,96,2,12,768]{4,2,3,0,1:T(2,128)(2,1)}), bf16[1,96,2,12,768]{4,2,3,0,1:T(2,128)(2,1)}, u32[]{:S(2)}, u32[]{:S(2)}) async-start(bf16[1,96,2,12,768]{4,2,3,0,1:T(2,128)(2,1)} %copy.157), calls=%async_computation.3 | async-start | bytes 7077888 | tf_op jit(solution)/shard_map/all_to_all | solution.py:204
  1247.2 84.9 %copy-start.7 = (bf16[1,12,180,768]{3,2,1,0:T(8,128)(2,1)S(1)}, bf16[1,12,180,768]{3,2,1,0:T(8,128)(2,1)}, u32[]{:S(2)}) copy-start(bf16[1,12,180,768]{3,2,1,0:T(8,128)(2,1)} %param.15) | copy-start | bytes 9953284
  1247.2 84.8 %copy-start.35 = (f32[12,180]{1,0:T(8,128)S(1)}, f32[12,180]{1,0:T(8,128)}, u32[]{:S(2)}) copy-start(f32[12,180]{1,0:T(8,128)} %copy-done.34) | copy-start | bytes 25924
  1247.2 84.8 %copy-start.37 = (f32[180,1,96]{2,0,1:T(8,128)S(1)}, f32[180,1,96]{2,0,1:T(8,128)}, u32[]{:S(2)}) copy-start(f32[180,1,96]{2,0,1:T(8,128)} %copy-done.36) | copy-start | bytes 207364
  1247.2 84.8 %copy-start.58 = (f32[12,180]{1,0:T(8,128)S(1)}, f32[12,180]{1,0:T(8,128)}, u32[]{:S(2)}) copy-start(f32[12,180]{1,0:T(8,128)} %copy-done.56) | copy-start | bytes 25924
  1247.2 84.8 %copy-start.67 = (f32[768]{0:T(1024)S(1)}, f32[768]{0:T(1024)}, u32[]{:S(2)}) copy-start(f32[768]{0:T(1024)} %param.18) | copy-start | bytes 9220
  (66 other events, 321.3 us)
Sparse Core Ops, SparseCore 0:
  613.1 613.1 all-reduce.6
  1229.1 348.6 all-reduce.8
